TPU v7x, 256 devices: a whole 4x4x8 slice. The times are simulated.
256 devices in a mesh: star: 8 (over x, core), row: 32 (over z, y).
Axes of the slice: x: 4, y: 4, z: 8, core: 2. Of those that a mesh axis runs over, the one named last changes fastest.
Arguments:
- feature_maps: bfloat16 [64, 1024, 1024], P(None, 'row'), may hold values from -6 to 6
- coef_table: bfloat16 [64, 64], replicated, may hold values from -0.119628906 to 0.119628906
- star_counts: int32 [8], replicated, may hold values from 1 to 12, 32 in all
- star_cells: int32 [8, 12], replicated, may hold values from 0 to 63
- star_bands: int32 [8, 12], replicated, may hold values from 0 to 7
- psf_cotangent: bfloat16 [96, 1024, 1024], P('star', 'row'), may hold values from -6 to 6
Outputs:
- map_grad: float32 [64, 1024, 1024], P('star', 'row')
- coef_grad: float32 [64, 64], replicated
Inputs may be any that keep to these rules, and one draw needn't show every extreme that they name: The live stars of group g fill its slots 0 to star_counts[g] - 1; the counts sum to 32, and some group has exactly 12.
All inputs are finite; a program needn't handle non-finite values.
Results may differ from a plain program's by a relative error of at most 0.008.
Values may be sent and summed in bfloat16 or wider, within the bound.
No kernel may reach another device: no remote copies, remote signals or barrier semaphores. Data moves between devices by JAX's collectives and lax.ppermute only.
A program may use at most 128 MiB of HBM per device.

v0:
```python
import jax
import jax.numpy as jnp
from jax import lax
from jax.sharding import PartitionSpec as P

BANDS = 8


def fourier_tables(pupil_size):
    index_row = jnp.arange(pupil_size, dtype=jnp.int32)
    products = index_row[:, None] * index_row[None, :] % pupil_size
    angles = 2.0 * jnp.pi / pupil_size * products.astype(jnp.float32)
    return (jnp.cos(angles).astype(jnp.bfloat16), (-jnp.sin(angles)).astype(jnp.bfloat16))


def aperture_rows(first_row, row_count, pupil_size):
    centre = 0.5 * (pupil_size - 1)
    row_pos = (first_row + jnp.arange(row_count, dtype=jnp.int32)).astype(jnp.float32) - centre
    col_pos = jnp.arange(pupil_size, dtype=jnp.int32).astype(jnp.float32) - centre
    radius = row_pos[:, None] * row_pos[:, None] + col_pos[None, :] * col_pos[None, :]
    return jnp.where(radius <= 0.25 * pupil_size * pupil_size, 1.0, 0.0).astype(jnp.float32)


def wave_numbers(band_ids):
    wavelength = 0.55 + 0.35 * band_ids.astype(jnp.float32) / (BANDS - 1)
    return 2.0 * jnp.pi / wavelength


def table_pick(values, indices):
    positions = jnp.arange(values.shape[0], dtype=jnp.int32)
    chosen = jnp.where(positions[None, :] == indices[:, None], values[None, :], 0)
    return jnp.sum(chosen, axis=1)


def per_device(feature_maps, coef_table, star_counts, star_cells, star_bands, psf_cotangent):
    groups = lax.axis_size("star")
    my_group = lax.axis_index("star")
    slot_count = psf_cotangent.shape[0]
    map_count, row_count, pupil_size = feature_maps.shape
    flat_cells = star_cells.reshape(-1)
    flat_bands = star_bands.reshape(-1)
    cell_count = coef_table.shape[0]
    within = jnp.arange(slot_count, dtype=jnp.int32)
    owner_group = jnp.zeros_like(within) + my_group
    live_mask = within < table_pick(star_counts, owner_group)
    owner_group, within, live_mask = (owner_group, within, live_mask)
    slot_index = owner_group * slot_count + within
    cell_ids = table_pick(flat_cells, slot_index)
    band_ids = table_pick(flat_bands, slot_index)
    cell_hot = cell_ids[:, None] == jnp.arange(cell_count, dtype=jnp.int32)[None, :]
    coef_rows = jnp.dot(
        cell_hot.astype(jnp.bfloat16), coef_table, preferred_element_type=jnp.float32
    ).astype(jnp.bfloat16)
    flat_maps = feature_maps.reshape(map_count, row_count * pupil_size)
    path_error = jnp.dot(coef_rows, flat_maps, preferred_element_type=jnp.float32).reshape(
        -1, row_count, pupil_size
    )
    wave_number = wave_numbers(band_ids)
    phase_angle = wave_number[:, None, None] * path_error
    aperture = aperture_rows(lax.axis_index("row") * row_count, row_count, pupil_size)
    cos_phase = jnp.cos(phase_angle)
    sin_phase = jnp.sin(phase_angle)
    pupil_field = jnp.stack([aperture * cos_phase, aperture * sin_phase], 1).astype(jnp.bfloat16)
    cos_table, sin_table = fourier_tables(pupil_size)
    inverse = 1.0 / pupil_size
    along_cos = jnp.einsum(
        "sarc,cv->sarv", pupil_field, cos_table, preferred_element_type=jnp.float32
    )
    along_sin = jnp.einsum(
        "sarc,cv->sarv", pupil_field, sin_table, preferred_element_type=jnp.float32
    )
    column_field = jnp.stack(
        [along_cos[:, 0] - along_sin[:, 1], along_sin[:, 0] + along_cos[:, 1]], 1
    ).astype(jnp.bfloat16)
    pieces = lax.all_to_all(column_field, "row", split_axis=3, concat_axis=2, tiled=True)
    row_cos = jnp.einsum("sarv,ru->savu", pieces, cos_table, preferred_element_type=jnp.float32)
    row_sin = jnp.einsum("sarv,ru->savu", pieces, sin_table, preferred_element_type=jnp.float32)
    real_part = (row_cos[:, 0] - row_sin[:, 1]) * inverse
    imag_part = (row_sin[:, 0] + row_cos[:, 1]) * inverse
    focal_field = jnp.stack([real_part, imag_part], 1)
    weight = jnp.where(live_mask, 2.0, 0.0).astype(jnp.float32)[:, None, None, None]
    focal_grad = (weight * psf_cotangent.astype(jnp.float32)[:, None] * focal_field).astype(
        jnp.bfloat16
    )
    back_cos = jnp.einsum(
        "savu,ur->savr", focal_grad, cos_table, preferred_element_type=jnp.float32
    )
    back_sin = jnp.einsum(
        "savu,ur->savr", focal_grad, sin_table, preferred_element_type=jnp.float32
    )
    spectrum_grad = jnp.stack(
        [(back_cos[:, 0] + back_sin[:, 1]) * inverse, (back_cos[:, 1] - back_sin[:, 0]) * inverse],
        1,
    ).astype(jnp.bfloat16)
    pieces = lax.all_to_all(spectrum_grad, "row", split_axis=3, concat_axis=2, tiled=True)
    col_cos = jnp.einsum("savr,vc->sarc", pieces, cos_table, preferred_element_type=jnp.float32)
    col_sin = jnp.einsum("savr,vc->sarc", pieces, sin_table, preferred_element_type=jnp.float32)
    pupil_grad = jnp.stack([col_cos[:, 0] + col_sin[:, 1], col_cos[:, 1] - col_sin[:, 0]], 1)
    phase_grad = aperture * (cos_phase * pupil_grad[:, 1] - sin_phase * pupil_grad[:, 0])
    path_grad = (
        (wave_number[:, None, None] * phase_grad)
        .astype(jnp.bfloat16)
        .reshape(-1, row_count * pupil_size)
    )
    map_scores = lax.dot_general(
        path_grad, flat_maps, (((1,), (1,)), ((), ())), preferred_element_type=jnp.float32
    )
    coef_part = lax.dot_general(
        cell_hot.astype(jnp.float32),
        map_scores * (1.0 / (8 * pupil_size)),
        (((0,), (0,)), ((), ())),
        precision=lax.Precision.HIGHEST,
    )
    coef_grad = lax.psum(coef_part, ("star", "row"))
    share = map_count // groups
    map_grad = lax.psum_scatter(
        lax.dot_general(
            coef_rows, path_grad, (((0,), (0,)), ((), ())), preferred_element_type=jnp.float32
        ),
        "star",
        scatter_dimension=0,
        tiled=True,
    )
    return (map_grad.reshape(share, row_count, pupil_size), coef_grad)


def solution(mesh):
    placed = (P(None, "row", None), P(), P(), P(), P(), P("star", "row", None))
    return jax.shard_map(
        per_device,
        mesh=mesh,
        in_specs=placed,
        out_specs=(P("star", "row", None), P()),
        check_vma=False,
    )
```

profile of v0, /device:TPU:1, one launch (start us, length us, event | category | flops | bytes accessed | tf_op | source)
XLA Modules:
  0.0 501.8 jit_solution(5607141360308045111)
XLA Ops:
  7.2 0.0 copy-start
  7.2 0.8 broadcast_in_dim.72
  8.0 0.8 broadcast_in_dim.75
  8.7 0.2 select_reduce_fusion
  9.0 0.0 copy-done
  9.0 0.2 convolution_convert_fusion
  9.2 6.7 %fusion.3 = f32[12,32,1024]{2,0,1:T(8,128)S(1)} fusion(bf16[12,64]{1,0:T(8,128)(2,1)S(1)} %convolution_convert_fusion, bf16[8,8,32,1024]{3,2,1,0:T(8,128)(2,1)} %bitcast.95), kind=kOutput, calls=%fused_computation.8 | convolution fusion | flops 50331648 | bytes 5768704 | tf_op jit(solution)/shard_map/dot_general | solution.py:55
  15.9 0.1 fusion.56
  16.0 8.4 %fusion.54 = (bf16[12,1,32,1024]{3,0,2,1:T(8,128)(2,1)S(1)}, bf16[12,1,32,1024]{3,0,2,1:T(8,128)(2,1)S(1)}) fusion(f32[12,32,1024]{2,0,1:T(8,128)S(1)} %fusion.3, f32[32,1024]{1,0:T(8,128)S(1)} %fusion.56, f32[12]{0:T(128)S(1)} %add_divide_fusion), kind=kLoop, calls=%fused_computation.67 | loop fusion | flops 1966080 | bytes 3276848 | tf_op jit(solution)/shard_map/stack | solution.py:63
  24.4 0.3 pad_maximum_fusion
  24.7 17.9 %fusion.28 = f32[12,2,32,1024]{3,2,1,0:T(8,128)S(1)} fusion(bf16[12,2,32,1024]{3,0,2,1:T(8,128)(2,1)S(1)} %pad_maximum_fusion), kind=kOutput, calls=%fused_computation.36 | convolution fusion | flops 1627389952 | bytes 4718592 | tf_op jit(solution)/shard_map/sarc,cv->sarv/dot_general | solution.py:69
  42.5 17.3 %fusion.36 = f32[12,2,32,1024]{3,2,1,0:T(8,128)S(1)} fusion(bf16[12,2,32,1024]{3,0,2,1:T(8,128)(2,1)S(1)} %pad_maximum_fusion), kind=kOutput, calls=%fused_computation.40 | convolution fusion | flops 1626341376 | bytes 4718592 | tf_op jit(solution)/shard_map/sarc,cv->sarv/dot_general | solution.py:66
  59.9 1.2 fusion.45
  61.1 1.3 pad_maximum_fusion.1
  62.4 15.1 %copy.45 = bf16[12,2,32,1024]{2,1,0,3:T(2,128)(2,1)} copy(bf16[12,2,32,1024]{3,2,1,0:T(8,128)(2,1)} %pad_maximum_fusion.1) | data formatting | bytes 3145728 | tf_op jit(solution)/shard_map/stack | solution.py:72
  77.5 13.8 %reshape.93 = bf16[32,2,12288]{2,1,0:T(2,128)(2,1)} reshape(bf16[1024,12,2,32]{3,2,1,0:T(2,128)(2,1)} %bitcast.93) | data formatting | bytes 3145728
  91.3 0.0 copy-start.6
  91.3 0.0 copy-start.5
  91.3 12.3 %all-to-all-start = ((bf16[32,2,12288]{2,1,0:T(2,128)(2,1)}), bf16[32,2,12288]{2,1,0:T(2,128)(2,1)}, u32[]{:S(2)}, u32[]{:S(2)}) async-start(bf16[32,2,12288]{2,1,0:T(2,128)(2,1)} %reshape.93), calls=%async_computation | async-start | bytes 3145728 | tf_op jit(solution)/shard_map/all_to_all | solution.py:75
  103.6 0.0 reduce-scatter.2.cloned.1.call-start
  103.7 0.0 copy-done.6
  103.7 0.1 select_reduce_fusion.2
  103.8 0.0 copy-done.5
  103.8 1.4 convert_multiply_fusion
  105.2 36.3 %all-to-all-done = bf16[32,2,12288]{2,1,0:T(2,128)(2,1)} async-done(((bf16[32,2,12288]{2,1,0:T(2,128)(2,1)}), bf16[32,2,12288]{2,1,0:T(2,128)(2,1)}, u32[]{:S(2)}, u32[]{:S(2)}) %all-to-all-start) | async-done | bytes 1572896 | tf_op jit(solution)/shard_map/all_to_all | solution.py:75
  141.5 14.3 %reshape.94 = bf16[1024,12,2,32]{3,2,1,0:T(2,128)(2,1)} reshape(bf16[32,2,12288]{2,1,0:T(2,128)(2,1)} %all-to-all-done) | data formatting | bytes 3145728
  155.7 9.5 %copy.107 = bf16[12,2,32,32,32]{2,3,4,1,0:T(8,128)(2,1)} copy(bf16[12,2,32,32,32]{2,1,0,4,3:T(2,128)(2,1)} %bitcast.89) | data formatting | bytes 3145728 | tf_op jit(solution)/shard_map/all_to_all | solution.py:75
  165.2 9.8 %all_to_all.29 = bf16[12,2,1024,32]{2,3,1,0:T(8,128)(2,1)} reshape(bf16[12,2,32,32,32]{3,2,4,1,0:T(8,128)(2,1)} %bitcast.90) | data formatting | bytes 3145728 | tf_op jit(solution)/shard_map/all_to_all | solution.py:75
  175.0 0.0 copy-start.3
  175.0 18.3 %fusion.26 = f32[12,2,32,1024]{3,2,1,0:T(8,128)S(1)} fusion(bf16[12,2,1024,32]{2,3,1,0:T(8,128)(2,1)} %all_to_all.29), kind=kOutput, calls=%fused_computation.35 | convolution fusion | flops 1627389952 | bytes 4718592 | tf_op jit(solution)/shard_map/sarv,ru->savu/dot_general | solution.py:77
  193.3 0.0 copy-done.3
  193.3 17.4 %fusion.34 = f32[12,2,32,1024]{3,2,1,0:T(8,128)S(1)} fusion(bf16[12,2,1024,32]{2,3,1,0:T(8,128)(2,1)S(1)} %copy-done.3), kind=kOutput, calls=%fused_computation.39 | convolution fusion | flops 1626341376 | bytes 4718592 | tf_op jit(solution)/shard_map/sarv,ru->savu/dot_general | solution.py:76
  210.7 0.0 copy-start.2
  210.7 1.0 fusion.43
  211.7 0.4 copy-done.2
  212.1 16.4 %fusion.32 = f32[12,2,32,1024]{3,2,1,0:T(8,128)S(1)} fusion(f32[12,1,32,1024]{3,2,1,0:T(8,128)S(1)} %get-tuple-element.15, f32[12,1,32,1024]{3,2,1,0:T(8,128)S(1)} %get-tuple-element.14, f32[12,32,1024]{2,1,0:T(8,128)S(1)} %copy-done.2), kind=kOutput, calls=%fused_computation.38 | convolution fusion | flops 1628700672 | bytes 7864320 | tf_op jit(solution)/shard_map/savu,ur->savr/dot_general | solution.py:85
  228.5 16.7 %fusion.24 = f32[12,2,32,1024]{3,2,1,0:T(8,128)S(1)} fusion(f32[12,1,32,1024]{3,2,1,0:T(8,128)S(1)} %get-tuple-element.15, f32[12,1,32,1024]{3,2,1,0:T(8,128)S(1)} %get-tuple-element.14, f32[12,32,1024]{2,1,0:T(8,128)S(1)} %copy-done.2), kind=kOutput, calls=%fused_computation.34 | convolution fusion | flops 1629749248 | bytes 7864320 | tf_op jit(solution)/shard_map/savu,ur->savr/dot_general | solution.py:88
  245.2 0.8 fusion.41
  246.0 1.3 pad_maximum_fusion.2
  247.2 15.1 %copy.47 = bf16[12,2,32,1024]{2,1,0,3:T(2,128)(2,1)} copy(bf16[12,2,32,1024]{3,2,1,0:T(8,128)(2,1)} %pad_maximum_fusion.2) | data formatting | bytes 3145728 | tf_op jit(solution)/shard_map/stack | solution.py:91
  262.3 14.2 %reshape.95 = bf16[32,2,12288]{2,1,0:T(2,128)(2,1)} reshape(bf16[1024,12,2,32]{3,2,1,0:T(2,128)(2,1)} %bitcast.94) | data formatting | bytes 3145728
  276.5 42.9 %all_to_all.36 = bf16[32,2,12288]{2,1,0:T(2,128)(2,1)} all-to-all(bf16[32,2,12288]{2,1,0:T(2,128)(2,1)} %reshape.95), channel_id=1, replica_groups=mesh['star'=8,'row'=32] {'row'}, dimensions={0} | all-to-all | bytes 3145728 | tf_op jit(solution)/shard_map/all_to_all | solution.py:95
  319.5 14.3 %reshape.96 = bf16[1024,12,2,32]{3,2,1,0:T(2,128)(2,1)} reshape(bf16[32,2,12288]{2,1,0:T(2,128)(2,1)} %all_to_all.36) | data formatting | bytes 3145728
  333.7 9.5 %copy.106 = bf16[12,2,32,32,32]{2,3,4,1,0:T(8,128)(2,1)} copy(bf16[12,2,32,32,32]{2,1,0,4,3:T(2,128)(2,1)} %bitcast.91) | data formatting | bytes 3145728 | tf_op jit(solution)/shard_map/all_to_all | solution.py:95
  343.2 9.8 %all_to_all.33 = bf16[12,2,1024,32]{2,3,1,0:T(8,128)(2,1)} reshape(bf16[12,2,32,32,32]{3,2,4,1,0:T(8,128)(2,1)} %bitcast.92) | data formatting | bytes 3145728 | tf_op jit(solution)/shard_map/all_to_all | solution.py:95
  353.0 0.0 copy-start.4
  353.0 18.3 %fusion.22 = f32[12,2,32,1024]{3,2,1,0:T(8,128)S(1)} fusion(bf16[12,2,1024,32]{2,3,1,0:T(8,128)(2,1)} %all_to_all.33), kind=kOutput, calls=%fused_computation.33 | convolution fusion | flops 1627389952 | bytes 4718592 | tf_op jit(solution)/shard_map/savr,vc->sarc/dot_general | solution.py:97
  371.3 0.0 copy-done.4
  371.3 17.0 %fusion.30 = f32[12,2,32,1024]{3,2,1,0:T(8,128)S(1)} fusion(bf16[12,2,1024,32]{2,3,1,0:T(8,128)(2,1)S(1)} %copy-done.4), kind=kOutput, calls=%fused_computation.37 | convolution fusion | flops 1626341376 | bytes 4718592 | tf_op jit(solution)/shard_map/savr,vc->sarc/dot_general | solution.py:96
  388.3 1.1 fusion.95
  389.4 11.4 %fusion.19 = bf16[12,32,1024]{2,0,1:T(8,128)(2,1)S(1)} fusion(f32[12,1,32,1024]{3,2,1,0:T(8,128)S(1)} %get-tuple-element.24, f32[12,1,32,1024]{3,2,1,0:T(8,128)S(1)} %get-tuple-element.19, f32[12,1,32,1024]{3,2,1,0:T(8,128)S(1)} %get-tuple-element.25, f32[12,1,32,1024]{3,2,1,0:T(8,128)S(1)} %get-tuple-element.18, f32[12,32,1024]{2,0,1:T(8,128)S(1)} %fusion.3, ...), kind=kLoop, calls=%fused_computation.29 | loop fusion | flops 3538944 | bytes 8781872 | tf_op jit(solution)/shard_map/convert_element_type | solution.py:102
  400.8 0.4 copy.53
  401.2 0.1 pad.8
  401.4 0.6 copy.64
  402.0 4.5 fusion.97
  406.5 0.0 reduce-scatter.2.cloned.1.call-update
  406.5 0.0 copy-start.1
  406.5 6.8 %fusion.51 = f32[12,64]{1,0:T(8,128)S(1)} fusion(bf16[12,32,1024]{2,0,1:T(8,128)(2,1)S(1)} %fusion.19, bf16[64,32,1024]{2,1,0:T(8,128)(2,1)} %param.6), kind=kOutput, calls=%fused_computation.65 | convolution fusion | flops 50332416 | bytes 4983808 | tf_op jit(solution)/shard_map/dot_general | solution.py:105
  413.3 0.3 fusion.57
  413.6 78.1 %psum.7 = f32[64,64]{1,0:T(8,128)} all-reduce(f32[64,64]{1,0:T(8,128)S(1)} %fusion.57), channel_id=1, replica_groups=mesh['star'=8,'row'=32] {'star','row'}, use_global_device_ids=true, to_apply=%region_4.5 | all-reduce | flops 4096 | bytes 32768 | tf_op jit(solution)/shard_map/psum | solution.py:114
  491.7 0.0 reduce-scatter.2.cloned.1.call-done
  491.7 2.8 copy.55
  494.5 0.0 copy-done.1
  (5 shorter events, 0.0 us)
Async XLA Ops:
  7.2 1.8 copy-start
  91.3 12.3 %copy-start.6 = (s32[8]{0:T(128)S(1)}, s32[8]{0:T(128)}, u32[]{:S(2)}) copy-start(s32[8]{0:T(128)} %param.8) | copy-start | bytes 100
  91.3 12.4 %copy-start.5 = (bf16[12,32,1024]{2,1,0:T(8,128)(2,1)S(1)}, bf16[12,32,1024]{2,1,0:T(8,128)(2,1)}, u32[]{:S(2)}) copy-start(bf16[12,32,1024]{2,1,0:T(8,128)(2,1)} %param.11) | copy-start | bytes 2359300
  91.3 50.2 %all-to-all-start = ((bf16[32,2,12288]{2,1,0:T(2,128)(2,1)}), bf16[32,2,12288]{2,1,0:T(2,128)(2,1)}, u32[]{:S(2)}, u32[]{:S(2)}) async-start(bf16[32,2,12288]{2,1,0:T(2,128)(2,1)} %reshape.93), calls=%async_computation | async-start | bytes 3145728 | tf_op jit(solution)/shard_map/all_to_all | solution.py:75
  103.6 388.1 %reduce-scatter.2.cloned.1.call-start = ((), (), s32[]{:S(2)}) async-start(), calls=%async_computation.3 | async-start | bytes 9437184 | tf_op jit(solution)/shard_map/reduce_scatter | solution.py:116
  175.0 18.3 %copy-start.3 = (bf16[12,2,1024,32]{2,3,1,0:T(8,128)(2,1)S(1)}, bf16[12,2,1024,32]{2,3,1,0:T(8,128)(2,1)}, u32[]{:S(2)}) copy-start(bf16[12,2,1024,32]{2,3,1,0:T(8,128)(2,1)} %all_to_all.29) | copy-start | bytes 4718596
  210.7 1.4 copy-start.2
  353.0 18.3 %copy-start.4 = (bf16[12,2,1024,32]{2,3,1,0:T(8,128)(2,1)S(1)}, bf16[12,2,1024,32]{2,3,1,0:T(8,128)(2,1)}, u32[]{:S(2)}) copy-start(bf16[12,2,1024,32]{2,3,1,0:T(8,128)(2,1)} %all_to_all.33) | copy-start | bytes 4718596
  406.5 88.0 %copy-start.1 = (bf16[64,64]{1,0:T(8,128)(2,1)S(1)}, bf16[64,64]{1,0:T(8,128)(2,1)}, u32[]{:S(2)}) copy-start(bf16[64,64]{1,0:T(8,128)(2,1)} %param.7) | copy-start | bytes 24580
Sparse Core Ops, SparseCore 0:
  406.6 54.6 reduce-scatter.1
where the time goes:
time: 509 us; the launch traced here: 502 us
  matrix products  158 us (31%)
  local copies, waits for them, and re-layouts  132 us (26%)
  blocking collectives  121 us (24%)
  waiting for transfers between devices  36.3 us (7%)
  other arithmetic  27.5 us (5%)
  between operations  14.7 us (3%)
  starting transfers between devices  12.3 us (2%)
    psum x1, blocking collectives, per_device(): coef_grad = lax.psum(coef_part, ('star', 'row'))  78.1 us
    unnamed x21, local copies, waits for them, and re-layouts  60.5 us
    all_to_all x1, blocking collectives, per_device(): lax.all_to_all(spectrum_grad, 'row', split_axis=3, concat_axis=2, tiled=T...  42.9 us
    all_to_all x1, waiting for transfers between devices, per_device(): lax.all_to_all(column_field, 'row', split_axis=3, concat_axis=2, tiled=True)  36.3 us
    all_to_all x2, local copies, waits for them, and re-layouts, per_device(): lax.all_to_all(column_field, 'row', split_axis=3, concat_axis=2, tiled=True)  19.3 us
    all_to_all x2, local copies, waits for them, and re-layouts, per_device(): lax.all_to_all(spectrum_grad, 'row', split_axis=3, concat_axis=2, tiled=T...  19.3 us
    dot_general x1, matrix products, per_device(): jnp.einsum('savr,vc->sarc', pieces, sin_table, preferred_element_type=jnp...  18.3 us
    dot_general x1, matrix products, per_device(): jnp.einsum('sarv,ru->savu', pieces, sin_table, preferred_element_type=jnp...  18.3 us
  transfers between devices with their start and end apart: 2, of which 1 were waited for; matrix products, arithmetic and copies ran while one was open for 2% of the time, Pallas kernels for 0%

commit v1 on v0

--- a/solution.py
+++ b/solution.py
@@ -111,7 +111,7 @@
         (((0,), (0,)), ((), ())),
         precision=lax.Precision.HIGHEST,
     )
-    coef_grad = lax.psum(coef_part, ("star", "row"))
+    coef_grad = lax.psum(lax.psum(coef_part, "star"), "row")
     share = map_count // groups
     map_grad = lax.psum_scatter(
         lax.dot_general(

time: 509 us -> 595 us (1.17)
  the two profiles are of different devices: /device:TPU:1 before, /device:TPU:0 now
where the time goes in v1:
time: 595 us; the launch traced here: 588 us
  blocking collectives  208 us (35%)
  matrix products  158 us (27%)
  local copies, waits for them, and re-layouts  132 us (22%)
  waiting for transfers between devices  37.5 us (6%)
  other arithmetic  27.5 us (5%)
  between operations  14.7 us (2%)
  starting transfers between devices  10 us (2%)
    psum x2, blocking collectives, per_device(): coef_grad = lax.psum(lax.psum(coef_part, 'star'), 'row')  163 us
    unnamed x21, local copies, waits for them, and re-layouts  60.5 us
    all_to_all x1, blocking collectives, per_device(): lax.all_to_all(spectrum_grad, 'row', split_axis=3, concat_axis=2, tiled=T...  45.1 us
    all_to_all x1, waiting for transfers between devices, per_device(): lax.all_to_all(column_field, 'row', split_axis=3, concat_axis=2, tiled=True)  37.5 us
    all_to_all x2, local copies, waits for them, and re-layouts, per_device(): lax.all_to_all(column_field, 'row', split_axis=3, concat_axis=2, tiled=True)  19.3 us
    all_to_all x2, local copies, waits for them, and re-layouts, per_device(): lax.all_to_all(spectrum_grad, 'row', split_axis=3, concat_axis=2, tiled=T...  19.3 us
    dot_general x1, matrix products, per_device(): jnp.einsum('sarv,ru->savu', pieces, sin_table, preferred_element_type=jnp...  18.3 us
    dot_general x1, matrix products, per_device(): jnp.einsum('savr,vc->sarc', pieces, sin_table, preferred_element_type=jnp...  18.3 us
  transfers between devices with their start and end apart: 2, of which 1 were waited for; matrix products, arithmetic and copies ran while one was open for 1% of the time, Pallas kernels for 0%

profile of v1, /device:TPU:0, one launch (start us, length us, event | category | flops | bytes accessed | tf_op | source)
XLA Modules:
  0.0 587.6 jit_solution(14479515206599340468)
XLA Ops:
  7.2 0.0 copy-start
  7.2 0.8 broadcast_in_dim.72
  8.0 0.8 broadcast_in_dim.75
  8.7 0.2 select_reduce_fusion
  9.0 0.0 copy-done
  9.0 0.2 convolution_convert_fusion
  9.2 6.7 %fusion.3 = f32[12,32,1024]{2,0,1:T(8,128)S(1)} fusion(bf16[12,64]{1,0:T(8,128)(2,1)S(1)} %convolution_convert_fusion, bf16[8,8,32,1024]{3,2,1,0:T(8,128)(2,1)} %bitcast.95), kind=kOutput, calls=%fused_computation.8 | convolution fusion | flops 50331648 | bytes 5768704 | tf_op jit(solution)/shard_map/dot_general | solution.py:55
  15.9 0.1 fusion.56
  16.0 8.4 %fusion.54 = (bf16[12,1,32,1024]{3,0,2,1:T(8,128)(2,1)S(1)}, bf16[12,1,32,1024]{3,0,2,1:T(8,128)(2,1)S(1)}) fusion(f32[12,32,1024]{2,0,1:T(8,128)S(1)} %fusion.3, f32[32,1024]{1,0:T(8,128)S(1)} %fusion.56, f32[12]{0:T(128)S(1)} %add_divide_fusion), kind=kLoop, calls=%fused_computation.67 | loop fusion | flops 1966080 | bytes 3276848 | tf_op jit(solution)/shard_map/stack | solution.py:63
  24.4 0.3 pad_maximum_fusion
  24.7 17.9 %fusion.28 = f32[12,2,32,1024]{3,2,1,0:T(8,128)S(1)} fusion(bf16[12,2,32,1024]{3,0,2,1:T(8,128)(2,1)S(1)} %pad_maximum_fusion), kind=kOutput, calls=%fused_computation.36 | convolution fusion | flops 1627389952 | bytes 4718592 | tf_op jit(solution)/shard_map/sarc,cv->sarv/dot_general | solution.py:69
  42.5 17.3 %fusion.36 = f32[12,2,32,1024]{3,2,1,0:T(8,128)S(1)} fusion(bf16[12,2,32,1024]{3,0,2,1:T(8,128)(2,1)S(1)} %pad_maximum_fusion), kind=kOutput, calls=%fused_computation.40 | convolution fusion | flops 1626341376 | bytes 4718592 | tf_op jit(solution)/shard_map/sarc,cv->sarv/dot_general | solution.py:66
  59.9 1.2 fusion.45
  61.1 1.3 pad_maximum_fusion.1
  62.4 15.1 %copy.45 = bf16[12,2,32,1024]{2,1,0,3:T(2,128)(2,1)} copy(bf16[12,2,32,1024]{3,2,1,0:T(8,128)(2,1)} %pad_maximum_fusion.1) | data formatting | bytes 3145728 | tf_op jit(solution)/shard_map/stack | solution.py:72
  77.5 13.8 %reshape.93 = bf16[32,2,12288]{2,1,0:T(2,128)(2,1)} reshape(bf16[1024,12,2,32]{3,2,1,0:T(2,128)(2,1)} %bitcast.93) | data formatting | bytes 3145728
  91.3 0.0 copy-start.6
  91.3 0.0 copy-start.5
  91.4 10.0 %all-to-all-start = ((bf16[32,2,12288]{2,1,0:T(2,128)(2,1)}), bf16[32,2,12288]{2,1,0:T(2,128)(2,1)}, u32[]{:S(2)}, u32[]{:S(2)}) async-start(bf16[32,2,12288]{2,1,0:T(2,128)(2,1)} %reshape.93), calls=%async_computation | async-start | bytes 3145728 | tf_op jit(solution)/shard_map/all_to_all | solution.py:75
  101.4 0.0 reduce-scatter.2.cloned.1.call-start
  101.4 0.0 copy-done.6
  101.4 0.1 select_reduce_fusion.2
  101.5 0.0 copy-done.5
  101.5 1.4 convert_multiply_fusion
  103.0 37.5 %all-to-all-done = bf16[32,2,12288]{2,1,0:T(2,128)(2,1)} async-done(((bf16[32,2,12288]{2,1,0:T(2,128)(2,1)}), bf16[32,2,12288]{2,1,0:T(2,128)(2,1)}, u32[]{:S(2)}, u32[]{:S(2)}) %all-to-all-start) | async-done | bytes 1572896 | tf_op jit(solution)/shard_map/all_to_all | solution.py:75
  140.5 14.3 %reshape.94 = bf16[1024,12,2,32]{3,2,1,0:T(2,128)(2,1)} reshape(bf16[32,2,12288]{2,1,0:T(2,128)(2,1)} %all-to-all-done) | data formatting | bytes 3145728
  154.7 9.5 %copy.107 = bf16[12,2,32,32,32]{2,3,4,1,0:T(8,128)(2,1)} copy(bf16[12,2,32,32,32]{2,1,0,4,3:T(2,128)(2,1)} %bitcast.89) | data formatting | bytes 3145728 | tf_op jit(solution)/shard_map/all_to_all | solution.py:75
  164.2 9.8 %all_to_all.29 = bf16[12,2,1024,32]{2,3,1,0:T(8,128)(2,1)} reshape(bf16[12,2,32,32,32]{3,2,4,1,0:T(8,128)(2,1)} %bitcast.90) | data formatting | bytes 3145728 | tf_op jit(solution)/shard_map/all_to_all | solution.py:75
  174.0 0.0 copy-start.3
  174.0 18.3 %fusion.26 = f32[12,2,32,1024]{3,2,1,0:T(8,128)S(1)} fusion(bf16[12,2,1024,32]{2,3,1,0:T(8,128)(2,1)} %all_to_all.29), kind=kOutput, calls=%fused_computation.35 | convolution fusion | flops 1627389952 | bytes 4718592 | tf_op jit(solution)/shard_map/sarv,ru->savu/dot_general | solution.py:77
  192.3 0.0 copy-done.3
  192.3 17.4 %fusion.34 = f32[12,2,32,1024]{3,2,1,0:T(8,128)S(1)} fusion(bf16[12,2,1024,32]{2,3,1,0:T(8,128)(2,1)S(1)} %copy-done.3), kind=kOutput, calls=%fused_computation.39 | convolution fusion | flops 1626341376 | bytes 4718592 | tf_op jit(solution)/shard_map/sarv,ru->savu/dot_general | solution.py:76
  209.7 0.0 copy-start.2
  209.7 1.0 fusion.43
  210.8 0.4 copy-done.2
  211.1 16.4 %fusion.32 = f32[12,2,32,1024]{3,2,1,0:T(8,128)S(1)} fusion(f32[12,1,32,1024]{3,2,1,0:T(8,128)S(1)} %get-tuple-element.15, f32[12,1,32,1024]{3,2,1,0:T(8,128)S(1)} %get-tuple-element.14, f32[12,32,1024]{2,1,0:T(8,128)S(1)} %copy-done.2), kind=kOutput, calls=%fused_computation.38 | convolution fusion | flops 1628700672 | bytes 7864320 | tf_op jit(solution)/shard_map/savu,ur->savr/dot_general | solution.py:85
  227.5 16.7 %fusion.24 = f32[12,2,32,1024]{3,2,1,0:T(8,128)S(1)} fusion(f32[12,1,32,1024]{3,2,1,0:T(8,128)S(1)} %get-tuple-element.15, f32[12,1,32,1024]{3,2,1,0:T(8,128)S(1)} %get-tuple-element.14, f32[12,32,1024]{2,1,0:T(8,128)S(1)} %copy-done.2), kind=kOutput, calls=%fused_computation.34 | convolution fusion | flops 1629749248 | bytes 7864320 | tf_op jit(solution)/shard_map/savu,ur->savr/dot_general | solution.py:88
  244.2 0.8 fusion.41
  245.0 1.3 pad_maximum_fusion.2
  246.3 15.1 %copy.47 = bf16[12,2,32,1024]{2,1,0,3:T(2,128)(2,1)} copy(bf16[12,2,32,1024]{3,2,1,0:T(8,128)(2,1)} %pad_maximum_fusion.2) | data formatting | bytes 3145728 | tf_op jit(solution)/shard_map/stack | solution.py:91
  261.4 14.2 %reshape.95 = bf16[32,2,12288]{2,1,0:T(2,128)(2,1)} reshape(bf16[1024,12,2,32]{3,2,1,0:T(2,128)(2,1)} %bitcast.94) | data formatting | bytes 3145728
  275.6 45.1 %all_to_all.36 = bf16[32,2,12288]{2,1,0:T(2,128)(2,1)} all-to-all(bf16[32,2,12288]{2,1,0:T(2,128)(2,1)} %reshape.95), channel_id=1, replica_groups=mesh['star'=8,'row'=32] {'row'}, dimensions={0} | all-to-all | bytes 3145728 | tf_op jit(solution)/shard_map/all_to_all | solution.py:95
  320.7 14.3 %reshape.96 = bf16[1024,12,2,32]{3,2,1,0:T(2,128)(2,1)} reshape(bf16[32,2,12288]{2,1,0:T(2,128)(2,1)} %all_to_all.36) | data formatting | bytes 3145728
  335.0 9.5 %copy.106 = bf16[12,2,32,32,32]{2,3,4,1,0:T(8,128)(2,1)} copy(bf16[12,2,32,32,32]{2,1,0,4,3:T(2,128)(2,1)} %bitcast.91) | data formatting | bytes 3145728 | tf_op jit(solution)/shard_map/all_to_all | solution.py:95
  344.5 9.8 %all_to_all.33 = bf16[12,2,1024,32]{2,3,1,0:T(8,128)(2,1)} reshape(bf16[12,2,32,32,32]{3,2,4,1,0:T(8,128)(2,1)} %bitcast.92) | data formatting | bytes 3145728 | tf_op jit(solution)/shard_map/all_to_all | solution.py:95
  354.2 0.0 copy-start.4
  354.3 18.3 %fusion.22 = f32[12,2,32,1024]{3,2,1,0:T(8,128)S(1)} fusion(bf16[12,2,1024,32]{2,3,1,0:T(8,128)(2,1)} %all_to_all.33), kind=kOutput, calls=%fused_computation.33 | convolution fusion | flops 1627389952 | bytes 4718592 | tf_op jit(solution)/shard_map/savr,vc->sarc/dot_general | solution.py:97
  372.5 0.0 copy-done.4
  372.5 17.0 %fusion.30 = f32[12,2,32,1024]{3,2,1,0:T(8,128)S(1)} fusion(bf16[12,2,1024,32]{2,3,1,0:T(8,128)(2,1)S(1)} %copy-done.4), kind=kOutput, calls=%fused_computation.37 | convolution fusion | flops 1626341376 | bytes 4718592 | tf_op jit(solution)/shard_map/savr,vc->sarc/dot_general | solution.py:96
  389.5 1.1 fusion.95
  390.7 11.4 %fusion.19 = bf16[12,32,1024]{2,0,1:T(8,128)(2,1)S(1)} fusion(f32[12,1,32,1024]{3,2,1,0:T(8,128)S(1)} %get-tuple-element.24, f32[12,1,32,1024]{3,2,1,0:T(8,128)S(1)} %get-tuple-element.19, f32[12,1,32,1024]{3,2,1,0:T(8,128)S(1)} %get-tuple-element.25, f32[12,1,32,1024]{3,2,1,0:T(8,128)S(1)} %get-tuple-element.18, f32[12,32,1024]{2,0,1:T(8,128)S(1)} %fusion.3, ...), kind=kLoop, calls=%fused_computation.29 | loop fusion | flops 3538944 | bytes 8781872 | tf_op jit(solution)/shard_map/convert_element_type | solution.py:102
  402.0 0.4 copy.53
  402.5 0.1 pad.8
  402.6 0.6 copy.64
  403.2 4.5 fusion.97
  407.7 0.0 reduce-scatter.2.cloned.1.call-update
  407.7 0.0 copy-start.1
  407.7 6.8 %fusion.51 = f32[12,64]{1,0:T(8,128)S(1)} fusion(bf16[12,32,1024]{2,0,1:T(8,128)(2,1)S(1)} %fusion.19, bf16[64,32,1024]{2,1,0:T(8,128)(2,1)} %param.6), kind=kOutput, calls=%fused_computation.65 | convolution fusion | flops 50332416 | bytes 4983808 | tf_op jit(solution)/shard_map/dot_general | solution.py:105
  414.5 0.3 fusion.57
  414.8 24.4 %psum.14 = f32[64,64]{1,0:T(8,128)S(1)} all-reduce(f32[64,64]{1,0:T(8,128)S(1)} %fusion.57), channel_id=1, replica_groups=mesh['star'=8,'row'=32] {'star'}, use_global_device_ids=true, to_apply=%region_4.5 | all-reduce | flops 4096 | bytes 32768 | tf_op jit(solution)/shard_map/psum | solution.py:114
  439.2 138.2 %psum.15 = f32[64,64]{1,0:T(8,128)} all-reduce(f32[64,64]{1,0:T(8,128)S(1)} %psum.14), channel_id=1, replica_groups=mesh['star'=8,'row'=32] {'row'}, use_global_device_ids=true, to_apply=%region_5.6 | all-reduce | flops 4096 | bytes 32768 | tf_op jit(solution)/shard_map/psum | solution.py:114
  577.5 0.0 reduce-scatter.2.cloned.1.call-done
  577.5 2.8 copy.55
  580.3 0.0 copy-done.1
  (5 shorter events, 0.0 us)
Async XLA Ops:
  7.2 1.8 copy-start
  91.3 10.1 %copy-start.6 = (s32[8]{0:T(128)S(1)}, s32[8]{0:T(128)}, u32[]{:S(2)}) copy-start(s32[8]{0:T(128)} %param.8) | copy-start | bytes 100
  91.3 10.2 %copy-start.5 = (bf16[12,32,1024]{2,1,0:T(8,128)(2,1)S(1)}, bf16[12,32,1024]{2,1,0:T(8,128)(2,1)}, u32[]{:S(2)}) copy-start(bf16[12,32,1024]{2,1,0:T(8,128)(2,1)} %param.11) | copy-start | bytes 2359300
  91.4 49.1 %all-to-all-start = ((bf16[32,2,12288]{2,1,0:T(2,128)(2,1)}), bf16[32,2,12288]{2,1,0:T(2,128)(2,1)}, u32[]{:S(2)}, u32[]{:S(2)}) async-start(bf16[32,2,12288]{2,1,0:T(2,128)(2,1)} %reshape.93), calls=%async_computation | async-start | bytes 3145728 | tf_op jit(solution)/shard_map/all_to_all | solution.py:75
  101.4 476.1 %reduce-scatter.2.cloned.1.call-start = ((), (), s32[]{:S(2)}) async-start(), calls=%async_computation.3 | async-start | bytes 9437184 | tf_op jit(solution)/shard_map/reduce_scatter | solution.py:116
  174.0 18.3 %copy-start.3 = (bf16[12,2,1024,32]{2,3,1,0:T(8,128)(2,1)S(1)}, bf16[12,2,1024,32]{2,3,1,0:T(8,128)(2,1)}, u32[]{:S(2)}) copy-start(bf16[12,2,1024,32]{2,3,1,0:T(8,128)(2,1)} %all_to_all.29) | copy-start | bytes 4718596
  209.7 1.4 copy-start.2
  354.2 18.3 %copy-start.4 = (bf16[12,2,1024,32]{2,3,1,0:T(8,128)(2,1)S(1)}, bf16[12,2,1024,32]{2,3,1,0:T(8,128)(2,1)}, u32[]{:S(2)}) copy-start(bf16[12,2,1024,32]{2,3,1,0:T(8,128)(2,1)} %all_to_all.33) | copy-start | bytes 4718596
  407.7 172.6 %copy-start.1 = (bf16[64,64]{1,0:T(8,128)(2,1)S(1)}, bf16[64,64]{1,0:T(8,128)(2,1)}, u32[]{:S(2)}) copy-start(bf16[64,64]{1,0:T(8,128)(2,1)} %param.7) | copy-start | bytes 24580
Sparse Core Ops, SparseCore 0:
  407.8 51.2 reduce-scatter.1
